TPU v7x, 512 devices: a whole 4x4x16 slice. The times are simulated.
512 devices in a mesh: row: 32 (over x, y, core), col: 16 (over z).
Axes of the slice: x: 4, y: 4, z: 16, core: 2. Of those that a mesh axis runs over, the one named last changes fastest.
Arguments:
- features: bfloat16 [3, 32, 128, 512], P(None, 'row', 'col'), may hold values from -6 to 6
Outputs:
- panels: float32 [3, 32, 128, 256], P(None, 'row')
- trailing: float32 [3, 32, 128, 6, 16, 128], P(None, 'row', None, None, 'col')
All inputs are finite; a program needn't handle non-finite values.
Results may differ from a plain program's by a relative error of at most 0.0003.
Values may be sent and summed in bfloat16 or wider, within the bound.
A program may use at most 64 MiB of HBM per device.

v0:
```python
import functools
import math

import jax
import jax.numpy as jnp
from jax import lax
from jax.experimental import pallas as pl
from jax.experimental.pallas import tpu as pltpu
from jax.sharding import PartitionSpec as P

MESH = pl.DeviceIdType.MESH

F = 512
F32 = jnp.float32
BF = jnp.bfloat16
IPI = 1.0 / math.pi
POLY = (1.5707963050, -0.2145988016, 0.0889789874, -0.0501743046,
        0.0308918810, -0.0170881256, 0.0066700901, -0.0012624911)
NT = (((1,), (1,)), ((), ()))
NN = (((1,), (0,)), ((), ()))
TN = (((0,), (0,)), ((), ()))


def dot(a, b, dims):
    return lax.dot_general(a, b, dims, preferred_element_type=F32)


def split(a):
    hi = a.astype(BF)
    return hi, (a - hi.astype(F32)).astype(BF)


def dot3(a, b, dims):
    return dot(a[0], b[0], dims) + (dot(a[0], b[1], dims) + dot(a[1], b[0], dims))


def half_angle(ax):
    y = jnp.maximum(1.0 - ax, 1e-30)
    s = y * lax.rsqrt(y)
    z = 1.0 + ax
    root = (s * IPI) * (z * lax.rsqrt(z))
    p = POLY[7] * IPI
    for c in POLY[6::-1]:
        p = p * ax + c * IPI
    return root, s * p


def ntk(gram, ur, uc, scale):
    t = gram * (ur * uc)
    root, w = half_angle(jnp.abs(t))
    h = jnp.where(t < 0.0, w, 1.0 - w)
    th = t * h
    jf = root + th
    theta = th + jf
    root2, w2 = half_angle(jnp.minimum(jf, 1.0))
    h2 = 1.0 - w2
    return (root2 + h2 * (theta + jf)) * scale


def squares(x):
    x = x.astype(F32)
    return split(x * x)


def col_form(sq):
    ones = jnp.ones((128, F), BF)
    return (dot(sq[0], ones, NT) + dot(sq[1], ones, NT)) * (1.0 / F) + 1e-6


def row_form(sq):
    ones = jnp.ones((8, F), BF)
    return (dot(ones, sq[0], NT) + dot(ones, sq[1], NT))[0:1] * (1.0 / F) + 1e-6


VLIM = 24 * 1024 * 1024


def at(ref, i):
    return ref[i * 128:(i + 1) * 128]


def tile(xa, qa, xb, qb, same):
    gram = dot(xa, xb, NT) * (1.0 / F)
    k = ntk(gram, lax.rsqrt(qa), lax.rsqrt(qb), jnp.sqrt(qa) * jnp.sqrt(qb))
    if same is False:
        return k
    ii = lax.broadcasted_iota(jnp.int32, (128, 128), 0)
    jj = lax.broadcasted_iota(jnp.int32, (128, 128), 1)
    eq = ii == jj if same is True else (ii == jj) & same
    return jnp.where(eq, gram + 2.0 * qa + 1.0, k)


NZ = 16
PANEL0 = 3
RING2, ROOT, RING4 = 9, 12, 18
LOOP = PANEL0 + NZ


def panel_kernel(B, x_ref, C, R, xp, qpr, w_hi, w_lo, Q, qpc, M,
                 lsem, zrecv, zsend, crecv, csend, cdir, qrecv, qplane, qz, qsib):
    r = lax.axis_index("row")
    z = lax.axis_index("col")
    core = r % 2
    y = (r // 2) % 4
    x = r // 8
    N = 256
    is_root = (x == 0) & (y == 0)

    def rid(xx, yy, cc):
        return (((xx + 4) % 4) * 4 + ((yy + 4) % 4)) * 2 + cc

    own = pltpu.make_async_copy(x_ref.at[:, 0], R.at[z], lsem)
    own.start()
    sibling = (r + 1 - 2 * core, z)
    others = [((r + k) % 32, z) for k in range(1, 32)]
    to_root = (2 * z + r // NZ, r % NZ)
    cb, co = core, r // 2
    from_z = (z + NZ * core, r // 2)
    alone = (to_root[0] == r) & (to_root[1] == z)

    plane = [(rid(x + k // 4, y + k % 4, core), z) for k in (10, 6, 14, 9, 11, 2, 8, 5, 7, 13, 15, 1, 3, 4, 12)]
    bar = pltpu.get_barrier_semaphore()

    def hello(p):
        pl.semaphore_signal(bar, inc=1, device_id=p, device_id_type=MESH)

    for p in [(r, (z + k) % NZ) for k in range(1, NZ)] + others:
        hello(p)

    @pl.when(alone)
    def _():
        pl.semaphore_wait(bar, NZ - 1 + 31)

    @pl.when(jnp.logical_not(alone))
    def _():
        hello(to_root)
        hello(from_z)
        pl.semaphore_wait(bar, NZ - 1 + 31 + 2)

    own.wait()

    def remote(src, dst, ssem, rsem, to):
        return pltpu.make_async_remote_copy(src_ref=src, dst_ref=dst, send_sem=ssem, recv_sem=rsem,
                                            device_id=to, device_id_type=MESH)

    mine = Q.at[core, z]

    @pl.when(is_root)
    def _():
        for k in range(15):
            remote(R.at[z, 0], mine, qplane.at[k], qrecv.at[core, z], plane[k]).start()
        pltpu.make_async_copy(R.at[z, 0], mine, qrecv.at[core, z]).start()

    @pl.when(alone)
    def _():
        pltpu.make_async_copy(R.at[z], C.at[r // NZ, z], crecv.at[r // NZ, z]).start()

    @pl.when(jnp.logical_not(alone))
    def _():
        remote(R.at[z], C.at[r // NZ, z], cdir, crecv.at[r // NZ, z], to_root).start()

    def zcopy(o, d, hops):
        return remote(R.at[o], R.at[o], zsend.at[(0 if d > 0 else 2) + hops - 1], zrecv.at[o],
                      (r, (z + d * hops + NZ) % NZ))

    def qwait(t, o):
        pltpu.make_async_copy(Q.at[t, o], Q.at[t, o], qrecv.at[t, o]).wait()

    def to_sibling(o):
        remote(Q.at[core, o], Q.at[core, o], qsib, qrecv.at[core, o], sibling).start()

    qwait(core, z)
    for k in (8, 7, 9, 6, 10, 5, 11, 4, 12, 3, 13, 2, 14, 1, 15):
        remote(mine, mine, qz.at[k - 1], qrecv.at[core, z], (r, (z + k) % NZ)).start()
    to_sibling(z)
    for hops in (2, 1):
        zcopy(z, 1, hops).start()
        zcopy(z, -1, hops).start()

    def seq(i):
        d = (i + 1) // 2
        return lax.rem(jnp.where(i % 2 == 1, z - d, z + d) + NZ, NZ)

    def panel_step(tau):
        i = tau - PANEL0

        @pl.when((i >= 1) & (i < NZ))
        def _():
            o = seq(i)
            qwait(core, o)
            to_sibling(o)

    def arrived(o):
        pltpu.make_async_copy(R.at[o], R.at[o], zrecv.at[o]).wait()

    def along_z(d):
        up, down = (z - d + NZ) % NZ, (z + d) % NZ
        arrived(up)
        if d < 8:
            zcopy(up, 1, 2).start()
            zcopy(up, 1, 1).start()
            arrived(down)
            if d < 6:
                zcopy(down, -1, 2).start()
            zcopy(down, -1, 1).start()
        arrived((z - d + 1 + NZ) % NZ)
        arrived((z + d - 1) % NZ)

    blk = C.at[cb, co]

    def cwait(b, o):
        pltpu.make_async_copy(C.at[b, o], C.at[b, o], crecv.at[b, o]).wait()

    def step(tau, carry):
        panel_step(tau)

        @pl.when(tau == RING2)
        def _():
            along_z(2)

        @pl.when(tau == ROOT)
        def _():
            cwait(cb, co)
            for k in range(31):
                remote(blk, blk, csend.at[k], crecv.at[cb, co], others[k]).start()

        @pl.when(tau == RING4)
        def _():
            along_z(4)

        return carry

    lax.fori_loop(0, LOOP, step, 0)

    def from_sibling(o, carry):
        qwait(1 - core, o)
        return carry

    lax.fori_loop(0, NZ, from_sibling, 0)

    for t in range(2):
        v = Q[t].reshape(128, F)
        xp[t * 128:(t + 1) * 128] = v
        sq = squares(v)
        qpc[t * 128:(t + 1) * 128] = col_form(sq)
        qpr[:, t * 128:(t + 1) * 128] = row_form(sq)

    for i in range(2):
        for t in range(2):
            M[i * 128:(i + 1) * 128, t * 128:(t + 1) * 128] = tile(
                at(xp, i), at(qpc, i), at(xp, t), qpr[:, t * 128:(t + 1) * 128], i == t)
    ri = lax.broadcasted_iota(jnp.int32, (N, N), 0)
    ci = lax.broadcasted_iota(jnp.int32, (N, N), 1)
    M[:, N:2 * N] = jnp.where(ri == ci, 1.0, 0.0)

    def after_block(n):
        if n == 2:
            along_z(6)
        if n == 6:
            along_z(8)

    sub = lax.broadcasted_iota(jnp.int32, (8, 128), 0)
    G = B // 8

    def wide(v):
        return jnp.broadcast_to(v, (8, 128))

    for n in range(N // B):
        lo = n * B
        hi = lo + B
        D = M[lo:hi, lo // 128 * 128:lo // 128 * 128 + 128]
        o = lo % 128
        col = [[wide(D[8 * g:8 * g + 8, o + k:o + k + 1]) if g >= k // 8 else None for g in range(G)]
               for k in range(B)]
        lanes = list(range(hi // 128, 2)) + list(range(2, 3 + (hi - 1) // 128))
        S = [[M[lo + 8 * g:lo + 8 * g + 8, 128 * v:128 * v + 128] for v in lanes] for g in range(G)]
        for k in range(B):
            gk = k // 8
            rs = wide(lax.rsqrt(col[k][gk])[k % 8:k % 8 + 1])
            c = [col[k][g] * rs if g >= gk else None for g in range(G)]
            for m in range(k + 1, B):
                f = wide(c[m // 8][m % 8:m % 8 + 1])
                for g in range(m // 8, G):
                    col[m][g] = col[m][g] - c[g] * f
            below = jnp.where(sub > k % 8, c[gk], 0.0)
            for v in range(len(lanes)):
                row = wide(S[gk][v][k % 8:k % 8 + 1]) * rs
                S[gk][v] = jnp.where(sub == k % 8, row, S[gk][v] - below * row)
                for g in range(gk + 1, G):
                    S[g][v] = S[g][v] - c[g] * row
        Y = [jnp.concatenate([S[g][v] for g in range(G)], axis=0) for v in range(len(lanes))]
        for v in range(len(lanes)):
            M[lo:hi, 128 * lanes[v]:128 * lanes[v] + 128] = Y[v]
        if hi < N:
            ys = [split(y) for y in Y]
            U = split(M[lo:hi, hi:N])
            for v in range(len(lanes)):
                cs = slice(128 * lanes[v], 128 * lanes[v] + 128)
                M[hi:, cs] = M[hi:, cs] - dot3(U, ys[v], TN)
        after_block(n)
    wf = split(M[:, N:])
    w_hi[...] = wf[0]
    w_lo[...] = wf[1]

    def sent(ref, sem):
        pltpu.make_async_copy(ref, ref, sem).wait()

    @pl.when(is_root)
    def _():
        for k in range(15):
            sent(mine, qplane.at[k])

    for k in range(15):
        sent(mine, qz.at[k])
    sent(Q.at[0], qsib)

    @pl.when(jnp.logical_not(alone))
    def _():
        sent(R.at[0], cdir)

    for k, n in ((0, 4), (1, 4), (2, 4), (3, 3)):
        sent(R.at[pl.ds(0, n)], zsend.at[k])
    for k in range(31):
        sent(blk, csend.at[k])

    def rest(o, carry):
        cwait(1 - cb, o)

        @pl.when(o != co)
        def _():
            cwait(cb, o)
        return carry

    lax.fori_loop(0, NZ, rest, 0)


def update_kernel(C, R, xp, qpr, w_hi, w_lo, out_l, out_t, xr, qr, kr, xc, qc, qcr, kc, oslot, osem):
    r = lax.axis_index("row")
    z = lax.axis_index("col")
    w = (w_hi[...], w_lo[...])
    for a in range(3):
        v = R[:, a].reshape(128, F)
        xr[a * 128:(a + 1) * 128] = v
        qr[a * 128:(a + 1) * 128] = col_form(squares(v))
        for t in range(2):
            kr[a * 128:(a + 1) * 128, t * 128:(t + 1) * 128] = tile(
                at(xr, a), at(qr, a), at(xp, t), qpr[:, t * 128:(t + 1) * 128], (r == t) if a == 0 else False)
    lr = dot3(split(kr[...]), w, NT)
    out_l[...] = lr
    for a in range(3):
        for b in range(2):
            t = 2 * a + b
            v = C[b, :, a].reshape(128, F)
            xc[t * 128:(t + 1) * 128] = v
            sq = squares(v)
            qc[t * 128:(t + 1) * 128] = col_form(sq)
            qcr[:, t * 128:(t + 1) * 128] = row_form(sq)
    for i in range(6):
        for t in range(2):
            kc[i * 128:(i + 1) * 128, t * 128:(t + 1) * 128] = tile(
                at(xc, i), at(qc, i), at(xp, t), qpr[:, t * 128:(t + 1) * 128],
                (z == t) if i == 0 else False)
    lc = split(dot3(split(kc[...]), w, NT))
    lr = split(lr)
    copies = []
    for a in range(3):
        rows = slice(a * 128, (a + 1) * 128)
        for t in range(6):
            cols = slice(t * 128, (t + 1) * 128)
            k = tile(at(xr, a), at(qr, a), at(xc, t), qcr[:, cols],
                     (r == z + NZ * (t % 2)) if t // 2 == a else False)
            k = k - dot3(tuple(v[rows] for v in lr), tuple(v[cols] for v in lc), NT)
            oslot[pl.ds(a * 768 + t, 128, stride=6), :] = k
        c = pltpu.make_async_copy(oslot.at[pl.ds(a * 768, 768)], out_t.at[pl.ds(a * 768, 768)], osem.at[a])
        c.start()
        copies.append(c)
    for c in copies:
        c.wait()


def local(features):
    dma = pltpu.SemaphoreType.DMA
    vm = pl.BlockSpec(memory_space=pltpu.VMEM)
    parts = pl.pallas_call(
        functools.partial(panel_kernel, 32),
        out_shape=(jax.ShapeDtypeStruct((2, NZ, 3, 8, F), BF), jax.ShapeDtypeStruct((NZ, 3, 8, F), BF),
                   jax.ShapeDtypeStruct((256, F), BF), jax.ShapeDtypeStruct((1, 256), F32),
                   jax.ShapeDtypeStruct((256, 256), BF), jax.ShapeDtypeStruct((256, 256), BF)),
        in_specs=[pl.BlockSpec(memory_space=pl.ANY)],
        out_specs=(vm,) * 6,
        scratch_shapes=[pltpu.VMEM((2, NZ, 8, F), BF),
                        pltpu.VMEM((256, 128), F32), pltpu.VMEM((256, 512), F32),
                        dma, dma((NZ,)), dma((4,)), dma((2, NZ)), dma((31,)), dma,
                        dma((2, NZ)), dma((15,)), dma((15,)), dma],
        compiler_params=pltpu.CompilerParams(collective_id=0, has_side_effects=True, vmem_limit_bytes=VLIM),
        name="panel_kernel",
    )(features)
    out_l, out_t = pl.pallas_call(
        update_kernel,
        out_shape=(jax.ShapeDtypeStruct((384, 256), F32), jax.ShapeDtypeStruct((2304, 128), F32)),
        in_specs=[vm] * 6,
        out_specs=(vm, pl.BlockSpec(memory_space=pl.ANY)),
        scratch_shapes=[pltpu.VMEM((384, F), BF), pltpu.VMEM((384, 128), F32), pltpu.VMEM((384, 256), F32),
                        pltpu.VMEM((768, F), BF), pltpu.VMEM((768, 128), F32), pltpu.VMEM((1, 768), F32),
                        pltpu.VMEM((768, 256), F32), pltpu.VMEM((2304, 128), F32), dma((3,))],
        compiler_params=pltpu.CompilerParams(vmem_limit_bytes=VLIM),
        name="update_kernel",
    )(*parts)
    return out_l.reshape(3, 1, 128, 256), out_t.reshape(3, 1, 128, 6, 1, 128)


def solution(mesh):
    return jax.shard_map(
        local,
        mesh=mesh,
        in_specs=(P(None, "row", "col", None),),
        out_specs=(P(None, "row", None, None), P(None, "row", None, None, "col", None)),
        check_vma=False,
    )
```

profile of v0, /device:TPU:25, one launch (start us, length us, event | category | flops | bytes accessed | tf_op | source)
XLA Modules:
  0.0 54.1 jit_solution(8593541790197624047)
XLA Ops:
  0.6 0.0 copy-start
  0.6 0.7 %copy-done = bf16[3,1,8,512]{3,2,1,0:T(8,128)(2,1)S(1)} copy-done((bf16[3,1,8,512]{3,2,1,0:T(8,128)(2,1)S(1)}, bf16[3,1,8,512]{3,2,1,0:T(8,128)(2,1)}, u32[]{:S(2)}) %copy-start) | copy-done | bytes 24600
  1.4 43.6 %panel_kernel.1 = (bf16[2,16,3,8,512]{4,3,2,1,0:T(8,128)(2,1)S(1)}, bf16[16,3,8,512]{3,2,1,0:T(8,128)(2,1)S(1)}, bf16[256,512]{1,0:T(8,128)(2,1)S(1)}, f32[1,256...) custom-call(bf16[3,1,8,512]{3,2,1,0:T(8,128)(2,1)S(1)} %copy-done), custom_call_target="tpu_custom_call" | custom-call | tf_op jit(solution)/shard_map/panel_kernel/pallas_call | solution.py:384
  45.0 9.0 %update_kernel.1 = (f32[384,256]{1,0:T(8,128)}, f32[2304,128]{1,0:T(8,128)}) custom-call(bf16[2,16,3,8,512]{4,3,2,1,0:T(8,128)(2,1)S(1)} %get-tuple-element.10.C, bf16[16,3,8,512]{3,2,1,0:T(8,128)(2,1)S(1)} %get-tuple-element.11.R, bf16[256,512]{1,0:T(8,128)(2,1)S(1)} %get-tuple-element.12.xp, f32[1,256]{1,0:T(1,128)S(1)} %get-tuple-element.13.qpr, ...), custom_call_target="tpu_custom_call" | custom-call | tf_op jit(solution)/shard_map/update_kernel/pallas_call | solution.py:398
Async XLA Ops:
  0.6 0.7 %copy-start = (bf16[3,1,8,512]{3,2,1,0:T(8,128)(2,1)S(1)}, bf16[3,1,8,512]{3,2,1,0:T(8,128)(2,1)}, u32[]{:S(2)}) copy-start(bf16[3,1,8,512]{3,2,1,0:T(8,128)(2,1)} %x_ref.1) | copy-start | bytes 73732
where the time goes:
time: 54.3 us; the launch traced here: 54.1 us
  Pallas kernels  52.6 us (97%)
  between operations  0.81 us (1%)
  local copies, waits for them, and re-layouts  0.73 us (1%)
    pallas_call x1, Pallas kernels, local(): pl.pallas_call(functools.partial(panel_kernel, 32), out_shape=(jax.ShapeD...  43.6 us
    pallas_call x1, Pallas kernels, local(): pl.pallas_call(update_kernel, out_shape=(jax.ShapeDtypeStruct((384, 256),...  8.98 us

commit v1 on v0

--- a/solution.py
+++ b/solution.py
@@ -97,7 +97,7 @@
 
 
 def panel_kernel(B, x_ref, C, R, xp, qpr, w_hi, w_lo, Q, qpc, M,
-                 lsem, zrecv, zsend, crecv, csend, cdir, qrecv, qplane, qz, qsib):
+                 lsem, zrecv, zsend, crecv, csend, cdir, csib, qrecv, qplane, qz, qsib):
     r = lax.axis_index("row")
     z = lax.axis_index("col")
     core = r % 2
@@ -112,7 +112,7 @@
     own = pltpu.make_async_copy(x_ref.at[:, 0], R.at[z], lsem)
     own.start()
     sibling = (r + 1 - 2 * core, z)
-    others = [((r + k) % 32, z) for k in range(1, 32)]
+    others = [((r + k) % 32, z) for k in range(2, 32, 2)] + [sibling]
     to_root = (2 * z + r // NZ, r % NZ)
     cb, co = core, r // 2
     from_z = (z + NZ * core, r // 2)
@@ -129,13 +129,13 @@
 
     @pl.when(alone)
     def _():
-        pl.semaphore_wait(bar, NZ - 1 + 31)
+        pl.semaphore_wait(bar, NZ - 1 + len(others))
 
     @pl.when(jnp.logical_not(alone))
     def _():
         hello(to_root)
         hello(from_z)
-        pl.semaphore_wait(bar, NZ - 1 + 31 + 2)
+        pl.semaphore_wait(bar, NZ - 1 + len(others) + 2)
 
     own.wait()
 
@@ -211,6 +211,12 @@
     def cwait(b, o):
         pltpu.make_async_copy(C.at[b, o], C.at[b, o], crecv.at[b, o]).wait()
 
+    def pass_on(k, carry):
+        o = (co + k) % NZ
+        cwait(cb, o)
+        remote(C.at[cb, o], C.at[cb, o], csib, crecv.at[cb, o], sibling).start()
+        return carry
+
     def step(tau, carry):
         panel_step(tau)
 
@@ -221,7 +227,7 @@
         @pl.when(tau == ROOT)
         def _():
             cwait(cb, co)
-            for k in range(31):
+            for k in range(16):
                 remote(blk, blk, csend.at[k], crecv.at[cb, co], others[k]).start()
 
         @pl.when(tau == RING4)
@@ -256,6 +262,8 @@
     def after_block(n):
         if n == 2:
             along_z(6)
+        if n == 4:
+            lax.fori_loop(1, NZ, pass_on, 0)
         if n == 6:
             along_z(8)
 
@@ -320,15 +328,12 @@
 
     for k, n in ((0, 4), (1, 4), (2, 4), (3, 3)):
         sent(R.at[pl.ds(0, n)], zsend.at[k])
-    for k in range(31):
+    for k in range(16):
         sent(blk, csend.at[k])
+    sent(C.at[cb, pl.ds(0, NZ - 1)], csib)
 
     def rest(o, carry):
         cwait(1 - cb, o)
-
-        @pl.when(o != co)
-        def _():
-            cwait(cb, o)
         return carry
 
     lax.fori_loop(0, NZ, rest, 0)
@@ -390,7 +395,7 @@
         out_specs=(vm,) * 6,
         scratch_shapes=[pltpu.VMEM((2, NZ, 8, F), BF),
                         pltpu.VMEM((256, 128), F32), pltpu.VMEM((256, 512), F32),
-                        dma, dma((NZ,)), dma((4,)), dma((2, NZ)), dma((31,)), dma,
+                        dma, dma((NZ,)), dma((4,)), dma((2, NZ)), dma((16,)), dma, dma,
                         dma((2, NZ)), dma((15,)), dma((15,)), dma],
         compiler_params=pltpu.CompilerParams(collective_id=0, has_side_effects=True, vmem_limit_bytes=VLIM),
         name="panel_kernel",

time: 54.3 us -> 53.4 us (0.983)
  the two profiles are of different devices: /device:TPU:25 before, /device:TPU:4 now
where the time goes in v1:
time: 53.4 us; the launch traced here: 53.3 us
  Pallas kernels  51.7 us (97%)
  between operations  0.81 us (2%)
  local copies, waits for them, and re-layouts  0.73 us (1%)
    pallas_call x1, Pallas kernels, local(): pl.pallas_call(functools.partial(panel_kernel, 32), out_shape=(jax.ShapeD...  42.8 us
    pallas_call x1, Pallas kernels, local(): pl.pallas_call(update_kernel, out_shape=(jax.ShapeDtypeStruct((384, 256),...  8.98 us

profile of v1, /device:TPU:4, one launch (start us, length us, event | category | flops | bytes accessed | tf_op | source)
XLA Modules:
  0.0 53.3 jit_solution(1381665037813744002)
XLA Ops:
  0.6 0.0 copy-start
  0.6 0.7 %copy-done = bf16[3,1,8,512]{3,2,1,0:T(8,128)(2,1)S(1)} copy-done((bf16[3,1,8,512]{3,2,1,0:T(8,128)(2,1)S(1)}, bf16[3,1,8,512]{3,2,1,0:T(8,128)(2,1)}, u32[]{:S(2)}) %copy-start) | copy-done | bytes 24600
  1.4 42.8 %panel_kernel.1 = (bf16[2,16,3,8,512]{4,3,2,1,0:T(8,128)(2,1)S(1)}, bf16[16,3,8,512]{3,2,1,0:T(8,128)(2,1)S(1)}, bf16[256,512]{1,0:T(8,128)(2,1)S(1)}, f32[1,256...) custom-call(bf16[3,1,8,512]{3,2,1,0:T(8,128)(2,1)S(1)} %copy-done), custom_call_target="tpu_custom_call" | custom-call | tf_op jit(solution)/shard_map/panel_kernel/pallas_call | solution.py:389
  44.1 9.0 %update_kernel.1 = (f32[384,256]{1,0:T(8,128)}, f32[2304,128]{1,0:T(8,128)}) custom-call(bf16[2,16,3,8,512]{4,3,2,1,0:T(8,128)(2,1)S(1)} %get-tuple-element.10.C, bf16[16,3,8,512]{3,2,1,0:T(8,128)(2,1)S(1)} %get-tuple-element.11.R, bf16[256,512]{1,0:T(8,128)(2,1)S(1)} %get-tuple-element.12.xp, f32[1,256]{1,0:T(1,128)S(1)} %get-tuple-element.13.qpr, ...), custom_call_target="tpu_custom_call" | custom-call | tf_op jit(solution)/shard_map/update_kernel/pallas_call | solution.py:403
Async XLA Ops:
  0.6 0.7 %copy-start = (bf16[3,1,8,512]{3,2,1,0:T(8,128)(2,1)S(1)}, bf16[3,1,8,512]{3,2,1,0:T(8,128)(2,1)}, u32[]{:S(2)}) copy-start(bf16[3,1,8,512]{3,2,1,0:T(8,128)(2,1)} %x_ref.1) | copy-start | bytes 73732
